TPU v7x, 128 devices: a whole 4x4x4 slice. The times are simulated.
128 devices in a mesh: ctx: 16 (over y_hi, z, core), head: 8 (over y_lo, x).
Axes of the slice: x: 4, y: 4 (y_hi: 2, y_lo: 2; y = y_hi * 2 + y_lo), z: 4, core: 2. Of those that a mesh axis runs over, the one named last changes fastest.
Arguments:
- queries: bfloat16 [16384, 4096], P('ctx', 'head'), may hold values from -24 to 24
- key_states: bfloat16 [16384, 4096], P('ctx', 'head'), may hold values from -24 to 24
- value_states: bfloat16 [16384, 4096], P('ctx', 'head'), may hold values from -6 to 6
- out_grad: bfloat16 [16384, 4096], P('ctx', 'head'), may hold values from -6 to 6
- selected: int32 [256, 16], P('ctx'), may hold values from -1 to 255, as said below
Outputs:
- query_grad: bfloat16 [16384, 4096], P(('ctx', 'head'))
- key_grad: bfloat16 [16384, 4096], P(('ctx', 'head'))
- value_grad: bfloat16 [16384, 4096], P(('ctx', 'head'))
Inputs may be any that keep to these rules, and one draw needn't show every extreme that they name: `selected`: row i holds 16 distinct entries, each a block index or -1; block i itself is always among them and every other block named comes before i. In the aligned groups of 16 rows, the blocks named that lie in another group's range number at most 1 for each other group, exactly 1 for every earlier group, and none for a later group.
All inputs are finite; a program needn't handle non-finite values.
Results may differ from a plain program's by a relative error of at most 0.011.
Values may be sent and summed in bfloat16 or wider, within the bound.
No kernel may reach another device: no remote copies, remote signals or barrier semaphores. Data moves between devices by JAX's collectives and lax.ppermute only.
A program may use at most 192 MiB of HBM per device.

v0:
```python
import jax
import jax.numpy as jnp
from jax import lax
from jax.sharding import PartitionSpec as P

HDIM = 128
HEAD_DEV = 4
BLOCK = 64
TOPK = 16
CAP = 1
GROUP = 8


def pack_slots(member, ranking, per_dev):
    slots = jnp.arange(CAP, dtype=jnp.int32)
    locals_idx = jnp.arange(per_dev, dtype=jnp.int32)
    picks = member[:, None, :] & (ranking[:, None, :] == slots[None, :, None])
    return jnp.sum(jnp.where(picks, locals_idx[None, None, :], 0), axis=2)


def group_grads(query_blk, key_blk, value_blk, grad_blk, select_blk, own_ids):
    count = query_blk.shape[0]
    scale = 1.0 / HDIM**0.5
    width = HEAD_DEV * HDIM
    query_h = query_blk.reshape(count, BLOCK, HEAD_DEV, HDIM)
    key_h = key_blk.reshape(count, TOPK * BLOCK, HEAD_DEV, HDIM)
    value_h = value_blk.reshape(count, TOPK * BLOCK, HEAD_DEV, HDIM)
    grad_h = grad_blk.reshape(count, BLOCK, HEAD_DEV, HDIM)
    key_idx = jnp.arange(TOPK * BLOCK, dtype=jnp.int32)
    slot_of = key_idx // BLOCK
    key_pos = key_idx % BLOCK
    query_pos = jnp.arange(BLOCK, dtype=jnp.int32)
    block_of = select_blk[:, slot_of]
    allowed = (block_of >= 0)[:, None, :] & (
        (block_of != own_ids[:, None])[:, None, :]
        | (key_pos[None, None, :] <= query_pos[None, :, None])
    )
    scores = (
        jnp.einsum("gqhd,gkhd->ghqk", query_h, key_h, preferred_element_type=jnp.float32) * scale
    )
    scores = jnp.where(allowed[:, None], scores, -1e30)
    highest = jnp.max(scores, axis=-1, keepdims=True)
    expo = jnp.exp(scores - highest)
    probs = expo / jnp.sum(expo, axis=-1, keepdims=True)
    probs_low = probs.astype(jnp.bfloat16)
    output = jnp.einsum("ghqk,gkhd->gqhd", probs_low, value_h, preferred_element_type=jnp.float32)
    delta = jnp.einsum("gqhd,gqhd->ghq", grad_h.astype(jnp.float32), output)
    dprobs = jnp.einsum("gqhd,gkhd->ghqk", grad_h, value_h, preferred_element_type=jnp.float32)
    dscores = probs * (dprobs - delta[..., None])
    dscores_low = dscores.astype(jnp.bfloat16)
    dquery = (
        jnp.einsum("ghqk,gkhd->gqhd", dscores_low, key_h, preferred_element_type=jnp.float32)
        * scale
    ).astype(jnp.bfloat16)
    dkey = (
        jnp.einsum("ghqk,gqhd->gkhd", dscores_low, query_h, preferred_element_type=jnp.float32)
        * scale
    )
    dvalue = jnp.einsum("ghqk,gqhd->gkhd", probs_low, grad_h, preferred_element_type=jnp.float32)
    return (
        dquery.reshape(count, BLOCK, width),
        dkey.reshape(count * TOPK, BLOCK, width),
        dvalue.reshape(count * TOPK, BLOCK, width),
    )


def per_device(queries, key_states, value_states, out_grad, selected):
    ranges = lax.axis_size("ctx")
    here = lax.axis_index("ctx")
    per_dev = selected.shape[0]
    width = queries.shape[1]
    range_ids = jnp.arange(ranges, dtype=jnp.int32)
    locals_idx = jnp.arange(per_dev, dtype=jnp.int32)
    usable = selected >= 0
    owner = jnp.where(usable, selected // per_dev, here)
    local_blk = jnp.where(usable, selected % per_dev, 0)
    hits = (owner[:, :, None, None] == range_ids[None, None, :, None]) & (
        local_blk[:, :, None, None] == locals_idx[None, None, None, :]
    )
    remote = usable & (owner != here)
    member = jnp.any(hits & remote[:, :, None, None], axis=(0, 1))
    ranking = jnp.cumsum(member.astype(jnp.int32), axis=1) - 1
    wanted_ids = pack_slots(member, ranking, per_dev)
    asks = lax.all_to_all(wanted_ids, "ctx", split_axis=0, concat_axis=0, tiled=True)
    key_blocks = key_states.reshape(per_dev, BLOCK, width)
    value_blocks = value_states.reshape(per_dev, BLOCK, width)
    sent_keys = key_blocks[asks]
    sent_values = value_blocks[asks]
    got_keys, got_values = (
        lax.all_to_all(sent_keys, "ctx", split_axis=0, concat_axis=0, tiled=True),
        lax.all_to_all(sent_values, "ctx", split_axis=0, concat_axis=0, tiled=True),
    )
    bank_keys = jnp.concatenate([key_blocks, got_keys.reshape(ranges * CAP, BLOCK, width)], axis=0)
    bank_values = jnp.concatenate(
        [value_blocks, got_values.reshape(ranges * CAP, BLOCK, width)], axis=0
    )
    rank_sel = jnp.sum(jnp.where(hits, ranking[None, None], 0), axis=(2, 3))
    bank_index = jnp.where(owner == here, local_blk, per_dev + owner * CAP + rank_sel)
    steps = per_dev // GROUP
    own_all = (here * per_dev + locals_idx).reshape(steps, GROUP)
    inputs = (
        queries.reshape(steps, GROUP, BLOCK, width),
        out_grad.reshape(steps, GROUP, BLOCK, width),
        bank_index.reshape(steps, GROUP, TOPK),
        selected.reshape(steps, GROUP, TOPK),
        own_all,
    )

    def advance(carry, item):
        grad_keys, grad_values = carry
        query_c, grad_c, index_c, select_c, own_c = item
        key_c = bank_keys[index_c].reshape(GROUP, TOPK * BLOCK, width)
        value_c = bank_values[index_c].reshape(GROUP, TOPK * BLOCK, width)
        dquery, dkey, dvalue = group_grads(query_c, key_c, value_c, grad_c, select_c, own_c)
        flat = index_c.reshape(-1)
        return ((grad_keys.at[flat].add(dkey), grad_values.at[flat].add(dvalue)), dquery)

    zeros = jnp.zeros((per_dev + ranges * CAP, BLOCK, width), jnp.float32)
    (grad_keys, grad_values), dquery = lax.scan(advance, (zeros, zeros), inputs)
    query_local = dquery.reshape(per_dev * BLOCK, width)
    back_keys, back_values = (
        lax.all_to_all(
            grad_keys[per_dev:].reshape(ranges, CAP, BLOCK, width),
            "ctx",
            split_axis=0,
            concat_axis=0,
            tiled=True,
        ),
        lax.all_to_all(
            grad_values[per_dev:].reshape(ranges, CAP, BLOCK, width),
            "ctx",
            split_axis=0,
            concat_axis=0,
            tiled=True,
        ),
    )
    flat_asks = asks.reshape(-1)
    key_total = grad_keys[:per_dev].at[flat_asks].add(back_keys.reshape(ranges * CAP, BLOCK, width))
    value_total = (
        grad_values[:per_dev].at[flat_asks].add(back_values.reshape(ranges * CAP, BLOCK, width))
    )
    key_local = key_total.reshape(per_dev * BLOCK, width).astype(jnp.bfloat16)
    value_local = value_total.reshape(per_dev * BLOCK, width).astype(jnp.bfloat16)
    query_out, key_out, value_out = (
        lax.all_to_all(query_local, "head", split_axis=0, concat_axis=1, tiled=True),
        lax.all_to_all(key_local, "head", split_axis=0, concat_axis=1, tiled=True),
        lax.all_to_all(value_local, "head", split_axis=0, concat_axis=1, tiled=True),
    )
    return (query_out, key_out, value_out)


def solution(mesh):
    return jax.shard_map(
        per_device,
        mesh=mesh,
        in_specs=(
            P("ctx", "head"),
            P("ctx", "head"),
            P("ctx", "head"),
            P("ctx", "head"),
            P("ctx", None),
        ),
        out_specs=(P(("ctx", "head"), None), P(("ctx", "head"), None), P(("ctx", "head"), None)),
        check_vma=False,
    )
```

profile of v0, /device:TPU:1, one launch (start us, length us, event | category | flops | bytes accessed | tf_op | source)
XLA Modules:
  0.0 779.9 jit_solution(9552881560634844395)
XLA Ops:
  3.8 16.2 %all_to_all.83 = s32[16,1,1]{2,1,0:T(1,128)S(1)} all-to-all(s32[16,1,1]{2,1,0:T(1,128)S(1)} %copy.83), channel_id=1, replica_groups=mesh['ctx'=16,'head'=8] {'ctx'}, dimensions={0} | all-to-all | bytes 128 | tf_op jit(solution)/shard_map/all_to_all | solution.py:84
  30.9 14.5 %all-to-all-done.1 = bf16[16,1,64,512]{3,2,1,0:T(8,128)(2,1)S(1)} async-done(((bf16[16,1,64,512]{3,2,1,0:T(8,128)(2,1)}), bf16[16,1,64,512]{3,2,1,0:T(8,128)(2,1)S(1)}, u32[]{:S(2)}, u32[]{:S(2)}) %all-to-all-start.1) | async-done | bytes 1048608 | tf_op jit(solution)/shard_map/all_to_all | solution.py:90
  57.2 10.6 %all-to-all-done.2 = bf16[16,1,64,512]{3,2,1,0:T(8,128)(2,1)} async-done(((bf16[16,1,64,512]{3,2,1,0:T(8,128)(2,1)}), bf16[16,1,64,512]{3,2,1,0:T(8,128)(2,1)}, u32[]{:S(2)}, u32[]{:S(2)}) %all-to-all-start.2) | async-done | bytes 1048608 | tf_op jit(solution)/shard_map/all_to_all | solution.py:91
  75.8 567.8 %while.16 = (s32[]{:T(128)}, f32[32,64,512]{2,1,0:T(8,128)}, f32[32,64,512]{2,1,0:T(8,128)}, bf16[2,8,64,512]{3,2,1,0:T(8,128)(2,1)}, s32[2,8,16]{2,1,0:T(8,128)...) while((s32[]{:T(128)}, f32[32,64,512]{2,1,0:T(8,128)}, ...), condition=%wide.region_9.10_spmd, body=%wide.region_4.9_spmd.sunk | while | flops 3265628928 | bytes 477484352 | solution.py:119
  108.5 12.5 %reshape.486 = bf16[8,1024,4,128]{3,2,1,0:T(4,128)(2,1)} reshape(bf16[128,64,512]{2,1,0:T(8,128)(2,1)} %gather_fusion.1) | data formatting | bytes 16777216 | tf_op jit(solution)/shard_map/while/body/eval_jaxpr/reshape;while/body/eval_jaxpr/reshape | solution.py:26
  129.0 12.5 %reshape.484 = bf16[8,1024,4,128]{3,2,1,0:T(4,128)(2,1)} reshape(bf16[128,64,512]{2,1,0:T(8,128)(2,1)} %gather_fusion) | data formatting | bytes 16777216 | tf_op jit(solution)/shard_map/while/body/eval_jaxpr/reshape;while/body/eval_jaxpr/reshape | solution.py:27
  151.3 12.6 %fusion.92 = (f32[8,4,64]{2,1,0:T(4,128)S(1)}, f32[8,4,64,1024]{3,2,1,0:T(8,128)}) fusion(f32[8,4,64,1024]{3,2,1,0:T(8,128)} %fusion.90, pred[8,64,1024]{2,1,0:T(8,128)(4,1)S(1)} %copy-done.1), kind=kOutput, calls=%fused_computation.100.clone.1 | output fusion | flops 12583935 | bytes 17309696 | tf_op jit(solution)/shard_map/while/body/eval_jaxpr/sub | solution.py:43
  169.3 12.1 %multiply_convert_fusion.2 = bf16[8,4,64,1024]{3,2,1,0:T(8,128)(2,1)} fusion(f32[8,4,64]{2,1,0:T(4,128)S(1)} %fusion.93, f32[8,4,64,1024]{3,2,1,0:T(8,128)} %get-tuple-element.277, f32[8,4,64]{2,1,0:T(4,128)S(1)} %get-tuple-element.278, bf16[8,1024,4,128]{3,2,1,0:T(4,128)(2,1)} %reshape.484, bf16[8,64,4,128]{3,2,1,0:T(4,128)(2,1)S(1)} %reshape.485), kind=kOutput, calls=%fused_computation.12.clone.1 | convolution fusion | flops 545259520 | bytes 21512192 | tf_op jit(solution)/shard_map/while/body/eval_jaxpr/gqhd,gkhd->ghqk/dot_general | solution.py:48
  192.8 11.5 %convolution_bitcast_fusion.2 = f32[8,1024,4,128]{1,3,2,0:T(8,128)} fusion(bf16[8,64,4,128]{3,2,1,0:T(4,128)(2,1)S(1)} %reshape.485, f32[8,4,64,1024]{3,2,1,0:T(8,128)} %get-tuple-element.277, f32[8,4,64]{2,1,0:T(4,128)S(1)} %get-tuple-element.278), kind=kOutput, calls=%fused_computation.11.clone.1 | convolution fusion | flops 541065216 | bytes 25698304 | tf_op jit(solution)/shard_map/while/body/eval_jaxpr/ghqk,gqhd->gkhd/dot_general | solution.py:59
  204.3 19.2 %copy.155 = f32[8,1024,4,128]{3,2,1,0:T(4,128)} copy(f32[8,1024,4,128]{1,3,2,0:T(8,128)} %convolution_bitcast_fusion.2) | data formatting | bytes 33554432 | tf_op jit(solution)/shard_map/while/body/eval_jaxpr/ghqk,gqhd->gkhd/transpose | solution.py:59
  223.5 19.9 %reshape.489 = f32[128,64,512]{2,1,0:T(8,128)} reshape(f32[8,1024,4,128]{3,2,1,0:T(4,128)} %copy.155) | data formatting | bytes 33554432 | tf_op jit(solution)/shard_map/while/body/eval_jaxpr/reshape | solution.py:63
  243.4 37.4 %scatter_fusion.1 = f32[32,64,512]{2,1,0:T(8,128)} fusion(f32[32,64,512]{2,1,0:T(8,128)} %get-tuple-element.293, s32[128]{0:T(128)S(1)} %fusion.89, f32[128,64,512]{2,1,0:T(8,128)} %reshape.489), kind=kCustom, calls=%fused_computation.6.clone.1 | custom fusion | flops 4194304 | bytes 50332160 | tf_op jit(solution)/shard_map/while/body/eval_jaxpr/scatter-add | solution.py:116
  291.1 19.2 %copy.154 = f32[8,1024,4,128]{3,2,1,0:T(4,128)} copy(f32[8,1024,4,128]{1,3,2,0:T(8,128)} %multiply_bitcast_fusion.2) | data formatting | bytes 33554432 | tf_op jit(solution)/shard_map/while/body/eval_jaxpr/mul | solution.py:56
  310.3 19.9 %reshape.488 = f32[128,64,512]{2,1,0:T(8,128)} reshape(f32[8,1024,4,128]{3,2,1,0:T(4,128)} %copy.154) | data formatting | bytes 33554432 | tf_op jit(solution)/shard_map/while/body/eval_jaxpr/reshape | solution.py:62
  330.3 37.2 %scatter_fusion = f32[32,64,512]{2,1,0:T(8,128)} fusion(f32[32,64,512]{2,1,0:T(8,128)} %get-tuple-element.292, s32[128]{0:T(128)S(1)} %fusion.89, f32[128,64,512]{2,1,0:T(8,128)} %reshape.488), kind=kCustom, calls=%fused_computation.5.clone.1 | custom fusion | flops 4194304 | bytes 50332160 | tf_op jit(solution)/shard_map/while/body/eval_jaxpr/scatter-add | solution.py:116
  383.2 12.5 %reshape.486 = bf16[8,1024,4,128]{3,2,1,0:T(4,128)(2,1)} reshape(bf16[128,64,512]{2,1,0:T(8,128)(2,1)} %gather_fusion.1) | data formatting | bytes 16777216 | tf_op jit(solution)/shard_map/while/body/eval_jaxpr/reshape;while/body/eval_jaxpr/reshape | solution.py:26
  403.8 12.5 %reshape.484 = bf16[8,1024,4,128]{3,2,1,0:T(4,128)(2,1)} reshape(bf16[128,64,512]{2,1,0:T(8,128)(2,1)} %gather_fusion) | data formatting | bytes 16777216 | tf_op jit(solution)/shard_map/while/body/eval_jaxpr/reshape;while/body/eval_jaxpr/reshape | solution.py:27
  426.1 12.6 %fusion.92 = (f32[8,4,64]{2,1,0:T(4,128)S(1)}, f32[8,4,64,1024]{3,2,1,0:T(8,128)}) fusion(f32[8,4,64,1024]{3,2,1,0:T(8,128)} %fusion.90, pred[8,64,1024]{2,1,0:T(8,128)(4,1)S(1)} %copy-done.1), kind=kOutput, calls=%fused_computation.100.clone.1 | output fusion | flops 12583935 | bytes 17309696 | tf_op jit(solution)/shard_map/while/body/eval_jaxpr/sub | solution.py:43
  444.1 12.1 %multiply_convert_fusion.2 = bf16[8,4,64,1024]{3,2,1,0:T(8,128)(2,1)} fusion(f32[8,4,64]{2,1,0:T(4,128)S(1)} %fusion.93, f32[8,4,64,1024]{3,2,1,0:T(8,128)} %get-tuple-element.277, f32[8,4,64]{2,1,0:T(4,128)S(1)} %get-tuple-element.278, bf16[8,1024,4,128]{3,2,1,0:T(4,128)(2,1)} %reshape.484, bf16[8,64,4,128]{3,2,1,0:T(4,128)(2,1)S(1)} %reshape.485), kind=kOutput, calls=%fused_computation.12.clone.1 | convolution fusion | flops 545259520 | bytes 21512192 | tf_op jit(solution)/shard_map/while/body/eval_jaxpr/gqhd,gkhd->ghqk/dot_general | solution.py:48
  467.6 11.5 %convolution_bitcast_fusion.2 = f32[8,1024,4,128]{1,3,2,0:T(8,128)} fusion(bf16[8,64,4,128]{3,2,1,0:T(4,128)(2,1)S(1)} %reshape.485, f32[8,4,64,1024]{3,2,1,0:T(8,128)} %get-tuple-element.277, f32[8,4,64]{2,1,0:T(4,128)S(1)} %get-tuple-element.278), kind=kOutput, calls=%fused_computation.11.clone.1 | convolution fusion | flops 541065216 | bytes 25698304 | tf_op jit(solution)/shard_map/while/body/eval_jaxpr/ghqk,gqhd->gkhd/dot_general | solution.py:59
  479.1 19.2 %copy.155 = f32[8,1024,4,128]{3,2,1,0:T(4,128)} copy(f32[8,1024,4,128]{1,3,2,0:T(8,128)} %convolution_bitcast_fusion.2) | data formatting | bytes 33554432 | tf_op jit(solution)/shard_map/while/body/eval_jaxpr/ghqk,gqhd->gkhd/transpose | solution.py:59
  498.3 19.9 %reshape.489 = f32[128,64,512]{2,1,0:T(8,128)} reshape(f32[8,1024,4,128]{3,2,1,0:T(4,128)} %copy.155) | data formatting | bytes 33554432 | tf_op jit(solution)/shard_map/while/body/eval_jaxpr/reshape | solution.py:63
  518.2 38.1 %scatter_fusion.1 = f32[32,64,512]{2,1,0:T(8,128)} fusion(f32[32,64,512]{2,1,0:T(8,128)} %get-tuple-element.293, s32[128]{0:T(128)S(1)} %fusion.89, f32[128,64,512]{2,1,0:T(8,128)} %reshape.489), kind=kCustom, calls=%fused_computation.6.clone.1 | custom fusion | flops 4194304 | bytes 50332160 | tf_op jit(solution)/shard_map/while/body/eval_jaxpr/scatter-add | solution.py:116
  566.6 19.2 %copy.154 = f32[8,1024,4,128]{3,2,1,0:T(4,128)} copy(f32[8,1024,4,128]{1,3,2,0:T(8,128)} %multiply_bitcast_fusion.2) | data formatting | bytes 33554432 | tf_op jit(solution)/shard_map/while/body/eval_jaxpr/mul | solution.py:56
  585.8 19.9 %reshape.488 = f32[128,64,512]{2,1,0:T(8,128)} reshape(f32[8,1024,4,128]{3,2,1,0:T(4,128)} %copy.154) | data formatting | bytes 33554432 | tf_op jit(solution)/shard_map/while/body/eval_jaxpr/reshape | solution.py:62
  605.7 37.8 %scatter_fusion = f32[32,64,512]{2,1,0:T(8,128)} fusion(f32[32,64,512]{2,1,0:T(8,128)} %get-tuple-element.292, s32[128]{0:T(128)S(1)} %fusion.89, f32[128,64,512]{2,1,0:T(8,128)} %reshape.488), kind=kCustom, calls=%fused_computation.5.clone.1 | custom fusion | flops 4194304 | bytes 50332160 | tf_op jit(solution)/shard_map/while/body/eval_jaxpr/scatter-add | solution.py:116
  652.7 10.8 %all-to-all-done.3 = bf16[8,128,512]{2,1,0:T(8,128)(2,1)S(1)} async-done(((bf16[8,128,512]{2,1,0:T(8,128)(2,1)}), bf16[8,128,512]{2,1,0:T(8,128)(2,1)S(1)}, u32[]{:S(2)}, u32[]{:S(2)}) %all-to-all-start.3) | async-done | bytes 1048608 | tf_op jit(solution)/shard_map/all_to_all | solution.py:145
  663.5 10.3 %all-to-all-start.4 = ((f32[16,1,64,512]{3,2,1,0:T(8,128)}), f32[16,1,64,512]{3,2,1,0:T(8,128)}, u32[]{:S(2)}, u32[]{:S(2)}) async-start(f32[16,1,64,512]{3,2,1,0:T(8,128)} %get-tuple-element.188), calls=%async_computation.4 | async-start | bytes 4194304 | tf_op jit(solution)/shard_map/all_to_all | solution.py:122
  678.0 24.4 %all-to-all-done.4 = f32[16,1,64,512]{3,2,1,0:T(8,128)} async-done(((f32[16,1,64,512]{3,2,1,0:T(8,128)}), f32[16,1,64,512]{3,2,1,0:T(8,128)}, u32[]{:S(2)}, u32[]{:S(2)}) %all-to-all-start.4) | async-done | bytes 2097184 | tf_op jit(solution)/shard_map/all_to_all | solution.py:122
  717.3 20.8 %all-to-all-done.6 = f32[16,1,64,512]{3,2,1,0:T(8,128)} async-done(((f32[16,1,64,512]{3,2,1,0:T(8,128)}), f32[16,1,64,512]{3,2,1,0:T(8,128)}, u32[]{:S(2)}, u32[]{:S(2)}) %all-to-all-start.6) | async-done | bytes 2097184 | tf_op jit(solution)/shard_map/all_to_all | solution.py:129
  747.1 11.1 %all-to-all-done.5 = bf16[8,128,512]{2,1,0:T(8,128)(2,1)} async-done(((bf16[8,128,512]{2,1,0:T(8,128)(2,1)}), bf16[8,128,512]{2,1,0:T(8,128)(2,1)}, u32[]{:S(2)}, u32[]{:S(2)}) %all-to-all-start.5) | async-done | bytes 1048608 | tf_op jit(solution)/shard_map/all_to_all | solution.py:146
  766.7 10.9 %all-to-all-done.7 = bf16[8,128,512]{2,1,0:T(8,128)(2,1)S(1)} async-done(((bf16[8,128,512]{2,1,0:T(8,128)(2,1)}), bf16[8,128,512]{2,1,0:T(8,128)(2,1)S(1)}, u32[]{:S(2)}, u32[]{:S(2)}) %all-to-all-start.7) | async-done | bytes 1048608 | tf_op jit(solution)/shard_map/all_to_all | solution.py:147
  (125 shorter events, 202.5 us)
Async XLA Ops:
  0.6 55.1 %copy-start.4 = (s32[16,16]{1,0:T(8,128)S(1)}, s32[16,16]{1,0:T(8,128)}, u32[]{:S(2)}) copy-start(s32[16,16]{1,0:T(8,128)} %param.11) | copy-start | bytes 3076
  0.6 55.1 %copy-start.2 = (bf16[1024,512]{1,0:T(8,128)(2,1)S(1)}, bf16[1024,512]{1,0:T(8,128)(2,1)}, u32[]{:S(2)}) copy-start(bf16[1024,512]{1,0:T(8,128)(2,1)} %param.8) | copy-start | bytes 3145732
  24.0 21.4 %all-to-all-start.1 = ((bf16[16,1,64,512]{3,2,1,0:T(8,128)(2,1)}), bf16[16,1,64,512]{3,2,1,0:T(8,128)(2,1)S(1)}, u32[]{:S(2)}, u32[]{:S(2)}) async-start(bf16[16,1,64,512]{3,2,1,0:T(8,128)(2,1)} %bitcast.19), calls=%async_computation.1 | async-start | bytes 2097152 | tf_op jit(solution)/shard_map/all_to_all | solution.py:90
  45.4 10.4 %copy-start.3 = (bf16[16,1,64,512]{3,2,1,0:T(8,128)(2,1)}, bf16[16,1,64,512]{3,2,1,0:T(8,128)(2,1)S(1)}, u32[]{:S(2)}) copy-start(bf16[16,1,64,512]{3,2,1,0:T(8,128)(2,1)S(1)} %all-to-all-done.1) | copy-start | bytes 3145732
  45.4 22.4 %all-to-all-start.2 = ((bf16[16,1,64,512]{3,2,1,0:T(8,128)(2,1)}), bf16[16,1,64,512]{3,2,1,0:T(8,128)(2,1)}, u32[]{:S(2)}, u32[]{:S(2)}) async-start(bf16[16,1,64,512]{3,2,1,0:T(8,128)(2,1)} %bitcast.23), calls=%async_computation.2 | async-start | bytes 2097152 | tf_op jit(solution)/shard_map/all_to_all | solution.py:91
  141.5 9.8 %copy-start.1 = (pred[8,64,1024]{2,1,0:T(8,128)(4,1)S(1)}, pred[8,64,1024]{2,1,0:T(8,128)(4,1)}, u32[]{:S(2)}) copy-start(pred[8,64,1024]{2,1,0:T(8,128)(4,1)} %or_and_fusion.2) | copy-start | bytes 1572868 | tf_op jit(solution)/shard_map/while
  141.5 22.3 %slice-start = ((s8[8388608]{0:T(1024)(128)(4,1)}), s8[4194304]{0:T(1024)(128)(4,1)S(1)}, s32[]{:S(2)}) async-start(s8[8388608]{0:T(1024)(128)(4,1)} %bitcast.97), calls=%async_computation.8 | async-start | bytes 8388608 | tf_op jit(solution)/shard_map/while
  151.3 12.6 %slice-start.1 = ((s8[8388608]{0:T(1024)(128)(4,1)}), s8[4194304]{0:T(1024)(128)(4,1)S(1)}, s32[]{:S(2)}) async-start(s8[8388608]{0:T(1024)(128)(4,1)} %bitcast.97), calls=%async_computation.9 | async-start | bytes 8388608 | tf_op jit(solution)/shard_map/while
  151.3 12.6 %copy-start = (f32[8,4,64,128]{3,1,2,0:T(4,128)S(1)}, f32[8,4,64,128]{3,1,2,0:T(4,128)}, u32[]{:S(2)}) copy-start(f32[8,4,64,128]{3,1,2,0:T(4,128)} %bitcast_convert_fusion.2) | copy-start | bytes 3145732 | tf_op jit(solution)/shard_map/while
  416.3 9.8 %copy-start.1 = (pred[8,64,1024]{2,1,0:T(8,128)(4,1)S(1)}, pred[8,64,1024]{2,1,0:T(8,128)(4,1)}, u32[]{:S(2)}) copy-start(pred[8,64,1024]{2,1,0:T(8,128)(4,1)} %or_and_fusion.2) | copy-start | bytes 1572868 | tf_op jit(solution)/shard_map/while
  416.3 22.3 %slice-start = ((s8[8388608]{0:T(1024)(128)(4,1)}), s8[4194304]{0:T(1024)(128)(4,1)S(1)}, s32[]{:S(2)}) async-start(s8[8388608]{0:T(1024)(128)(4,1)} %bitcast.97), calls=%async_computation.8 | async-start | bytes 8388608 | tf_op jit(solution)/shard_map/while
  426.1 12.6 %slice-start.1 = ((s8[8388608]{0:T(1024)(128)(4,1)}), s8[4194304]{0:T(1024)(128)(4,1)S(1)}, s32[]{:S(2)}) async-start(s8[8388608]{0:T(1024)(128)(4,1)} %bitcast.97), calls=%async_computation.9 | async-start | bytes 8388608 | tf_op jit(solution)/shard_map/while
  426.1 12.6 %copy-start = (f32[8,4,64,128]{3,1,2,0:T(4,128)S(1)}, f32[8,4,64,128]{3,1,2,0:T(4,128)}, u32[]{:S(2)}) copy-start(f32[8,4,64,128]{3,1,2,0:T(4,128)} %bitcast_convert_fusion.2) | copy-start | bytes 3145732 | tf_op jit(solution)/shard_map/while
  643.5 20.0 %all-to-all-start.3 = ((bf16[8,128,512]{2,1,0:T(8,128)(2,1)}), bf16[8,128,512]{2,1,0:T(8,128)(2,1)S(1)}, u32[]{:S(2)}, u32[]{:S(2)}) async-start(bf16[8,128,512]{2,1,0:T(8,128)(2,1)} %bitcast.109), calls=%async_computation.3 | async-start | bytes 2097152 | tf_op jit(solution)/shard_map/all_to_all | solution.py:145
  663.5 46.0 %copy-start.5 = (s32[16]{0:T(128)S(1)}, s32[16]{0:T(128)}, u32[]{:S(2)}) copy-start(s32[16]{0:T(128)} %get-tuple-element.154) | copy-start | bytes 196
  663.5 38.9 %all-to-all-start.4 = ((f32[16,1,64,512]{3,2,1,0:T(8,128)}), f32[16,1,64,512]{3,2,1,0:T(8,128)}, u32[]{:S(2)}, u32[]{:S(2)}) async-start(f32[16,1,64,512]{3,2,1,0:T(8,128)} %get-tuple-element.188), calls=%async_computation.4 | async-start | bytes 4194304 | tf_op jit(solution)/shard_map/all_to_all | solution.py:122
  702.4 35.7 %all-to-all-start.6 = ((f32[16,1,64,512]{3,2,1,0:T(8,128)}), f32[16,1,64,512]{3,2,1,0:T(8,128)}, u32[]{:S(2)}, u32[]{:S(2)}) async-start(f32[16,1,64,512]{3,2,1,0:T(8,128)} %get-tuple-element.186), calls=%async_computation.6 | async-start | bytes 4194304 | tf_op jit(solution)/shard_map/all_to_all | solution.py:129
  738.1 20.1 %all-to-all-start.5 = ((bf16[8,128,512]{2,1,0:T(8,128)(2,1)}), bf16[8,128,512]{2,1,0:T(8,128)(2,1)}, u32[]{:S(2)}, u32[]{:S(2)}) async-start(bf16[8,128,512]{2,1,0:T(8,128)(2,1)} %bitcast.31), calls=%async_computation.5 | async-start | bytes 2097152 | tf_op jit(solution)/shard_map/all_to_all | solution.py:146
  758.2 19.3 %all-to-all-start.7 = ((bf16[8,128,512]{2,1,0:T(8,128)(2,1)}), bf16[8,128,512]{2,1,0:T(8,128)(2,1)S(1)}, u32[]{:S(2)}, u32[]{:S(2)}) async-start(bf16[8,128,512]{2,1,0:T(8,128)(2,1)} %bitcast.36), calls=%async_computation.7 | async-start | bytes 2097152 | tf_op jit(solution)/shard_map/all_to_all | solution.py:147
where the time goes:
time: 790 us; the launch traced here: 780 us
  local copies, waits for them, and re-layouts  286 us (36%)
  other arithmetic  207 us (26%)
  matrix products  111 us (14%)
  waiting for transfers between devices  103 us (13%)
  starting transfers between devices  38.5 us (5%)
  loops' own time  17.4 us (2%)
  blocking collectives  16.2 us (2%)
    scatter-add x2, other arithmetic, advance(): grad_values.at[flat].add(dvalue)  75.6 us
    scatter-add x2, other arithmetic, advance(): grad_keys.at[flat].add(dkey)  74.9 us
    reshape x2, local copies, waits for them, and re-layouts, group_grads(): dvalue.reshape(count * TOPK, BLOCK, width)  39.8 us
    reshape x2, local copies, waits for them, and re-layouts, group_grads(): dkey.reshape(count * TOPK, BLOCK, width)  39.8 us
    transpose x2, local copies, waits for them, and re-layouts, group_grads(): jnp.einsum('ghqk,gqhd->gkhd', probs_low, grad_h, preferred_element_type=j...  38.4 us
    mul x2, local copies, waits for them, and re-layouts, group_grads(): jnp.einsum('ghqk,gqhd->gkhd', dscores_low, query_h, preferred_element_typ...  38.4 us
    sub x2, other arithmetic, group_grads(): expo = jnp.exp(scores - highest)  25.1 us
    reshape x2, local copies, waits for them, and re-layouts, group_grads(): key_h = key_blk.reshape(count, TOPK * BLOCK, HEAD_DEV, HDIM)  25.1 us
  transfers between devices with their start and end apart: 7, of which 7 were waited for; matrix products, arithmetic and copies ran while one was open for 5% of the time, Pallas kernels for 0%

commit v1 on v0

--- a/solution.py
+++ b/solution.py
@@ -143,7 +143,15 @@
     value_local = value_total.reshape(per_dev * BLOCK, width).astype(jnp.bfloat16)
     query_out, key_out, value_out = (
         lax.all_to_all(query_local, "head", split_axis=0, concat_axis=1, tiled=True),
-        lax.all_to_all(key_local, "head", split_axis=0, concat_axis=1, tiled=True),
+        jnp.concatenate(
+            jax.lax.all_to_all(
+                jnp.stack(jnp.split(key_local, jax.lax.psum(1, axis_name="head"), axis=0)),
+                axis_name="head",
+                split_axis=0,
+                concat_axis=0,
+            ),
+            1,
+        ),
         lax.all_to_all(value_local, "head", split_axis=0, concat_axis=1, tiled=True),
     )
     return (query_out, key_out, value_out)

time: 790 us -> 790 us (level)
  no operation moved by 1% of the time
where the time goes in v1:
time: 790 us; the launch traced here: 780 us
  local copies, waits for them, and re-layouts  291 us (37%)
  other arithmetic  206 us (26%)
  matrix products  111 us (14%)
  waiting for transfers between devices  98.6 us (12%)
  starting transfers between devices  38.5 us (5%)
  loops' own time  17.4 us (2%)
  blocking collectives  16.2 us (2%)
    scatter-add x2, other arithmetic, advance(): grad_values.at[flat].add(dvalue)  75.6 us
    scatter-add x2, other arithmetic, advance(): grad_keys.at[flat].add(dkey)  74.9 us
    reshape x2, local copies, waits for them, and re-layouts, group_grads(): dvalue.reshape(count * TOPK, BLOCK, width)  39.8 us
    reshape x2, local copies, waits for them, and re-layouts, group_grads(): dkey.reshape(count * TOPK, BLOCK, width)  39.8 us
    transpose x2, local copies, waits for them, and re-layouts, group_grads(): jnp.einsum('ghqk,gqhd->gkhd', probs_low, grad_h, preferred_element_type=j...  38.4 us
    mul x2, local copies, waits for them, and re-layouts, group_grads(): jnp.einsum('ghqk,gqhd->gkhd', dscores_low, query_h, preferred_element_typ...  38.4 us
    sub x2, other arithmetic, group_grads(): expo = jnp.exp(scores - highest)  25.1 us
    reshape x2, local copies, waits for them, and re-layouts, group_grads(): key_h = key_blk.reshape(count, TOPK * BLOCK, HEAD_DEV, HDIM)  25.1 us
  transfers between devices with their start and end apart: 7, of which 7 were waited for; matrix products, arithmetic and copies ran while one was open for 5% of the time, Pallas kernels for 0%

profile of v1, /device:TPU:1, one launch (start us, length us, event | category | flops | bytes accessed | tf_op | source)
XLA Modules:
  0.0 779.9 jit_solution(1943042083959756693)
XLA Ops:
  3.8 16.2 %all_to_all.72 = s32[16,1,1]{2,1,0:T(1,128)S(1)} all-to-all(s32[16,1,1]{2,1,0:T(1,128)S(1)} %copy.97), channel_id=1, replica_groups=mesh['ctx'=16,'head'=8] {'ctx'}, dimensions={0} | all-to-all | bytes 128 | tf_op jit(solution)/shard_map/all_to_all | solution.py:84
  30.9 14.5 %all-to-all-done.1 = bf16[16,1,64,512]{3,2,1,0:T(8,128)(2,1)S(1)} async-done(((bf16[16,1,64,512]{3,2,1,0:T(8,128)(2,1)}), bf16[16,1,64,512]{3,2,1,0:T(8,128)(2,1)S(1)}, u32[]{:S(2)}, u32[]{:S(2)}) %all-to-all-start.1) | async-done | bytes 1048608 | tf_op jit(solution)/shard_map/all_to_all | solution.py:90
  57.2 10.6 %all-to-all-done.2 = bf16[16,1,64,512]{3,2,1,0:T(8,128)(2,1)} async-done(((bf16[16,1,64,512]{3,2,1,0:T(8,128)(2,1)}), bf16[16,1,64,512]{3,2,1,0:T(8,128)(2,1)}, u32[]{:S(2)}, u32[]{:S(2)}) %all-to-all-start.2) | async-done | bytes 1048608 | tf_op jit(solution)/shard_map/all_to_all | solution.py:91
  75.8 567.8 %while.16 = (s32[]{:T(128)}, f32[32,64,512]{2,1,0:T(8,128)}, f32[32,64,512]{2,1,0:T(8,128)}, bf16[2,8,64,512]{3,2,1,0:T(8,128)(2,1)}, s32[2,8,16]{2,1,0:T(8,128)...) while((s32[]{:T(128)}, f32[32,64,512]{2,1,0:T(8,128)}, ...), condition=%wide.region_9.10_spmd, body=%wide.region_4.9_spmd.sunk | while | flops 3265628928 | bytes 477484352 | solution.py:119
  108.5 12.5 %reshape.506 = bf16[8,1024,4,128]{3,2,1,0:T(4,128)(2,1)} reshape(bf16[128,64,512]{2,1,0:T(8,128)(2,1)} %gather_fusion.1) | data formatting | bytes 16777216 | tf_op jit(solution)/shard_map/while/body/eval_jaxpr/reshape;while/body/eval_jaxpr/reshape | solution.py:26
  129.0 12.5 %reshape.504 = bf16[8,1024,4,128]{3,2,1,0:T(4,128)(2,1)} reshape(bf16[128,64,512]{2,1,0:T(8,128)(2,1)} %gather_fusion) | data formatting | bytes 16777216 | tf_op jit(solution)/shard_map/while/body/eval_jaxpr/reshape;while/body/eval_jaxpr/reshape | solution.py:27
  151.3 12.6 %fusion.93 = (f32[8,4,64]{2,1,0:T(4,128)S(1)}, f32[8,4,64,1024]{3,2,1,0:T(8,128)}) fusion(f32[8,4,64,1024]{3,2,1,0:T(8,128)} %fusion.91, pred[8,64,1024]{2,1,0:T(8,128)(4,1)S(1)} %copy-done.1), kind=kOutput, calls=%fused_computation.108.clone.1 | output fusion | flops 12583935 | bytes 17309696 | tf_op jit(solution)/shard_map/while/body/eval_jaxpr/sub | solution.py:43
  169.3 12.1 %multiply_convert_fusion.2 = bf16[8,4,64,1024]{3,2,1,0:T(8,128)(2,1)} fusion(f32[8,4,64]{2,1,0:T(4,128)S(1)} %fusion.94, f32[8,4,64,1024]{3,2,1,0:T(8,128)} %get-tuple-element.285, f32[8,4,64]{2,1,0:T(4,128)S(1)} %get-tuple-element.286, bf16[8,1024,4,128]{3,2,1,0:T(4,128)(2,1)} %reshape.504, bf16[8,64,4,128]{3,2,1,0:T(4,128)(2,1)S(1)} %reshape.505), kind=kOutput, calls=%fused_computation.12.clone.1 | convolution fusion | flops 545259520 | bytes 21512192 | tf_op jit(solution)/shard_map/while/body/eval_jaxpr/gqhd,gkhd->ghqk/dot_general | solution.py:48
  192.8 11.5 %convolution_bitcast_fusion.2 = f32[8,1024,4,128]{1,3,2,0:T(8,128)} fusion(bf16[8,64,4,128]{3,2,1,0:T(4,128)(2,1)S(1)} %reshape.505, f32[8,4,64,1024]{3,2,1,0:T(8,128)} %get-tuple-element.285, f32[8,4,64]{2,1,0:T(4,128)S(1)} %get-tuple-element.286), kind=kOutput, calls=%fused_computation.11.clone.1 | convolution fusion | flops 541065216 | bytes 25698304 | tf_op jit(solution)/shard_map/while/body/eval_jaxpr/ghqk,gqhd->gkhd/dot_general | solution.py:59
  204.3 19.2 %copy.169 = f32[8,1024,4,128]{3,2,1,0:T(4,128)} copy(f32[8,1024,4,128]{1,3,2,0:T(8,128)} %convolution_bitcast_fusion.2) | data formatting | bytes 33554432 | tf_op jit(solution)/shard_map/while/body/eval_jaxpr/ghqk,gqhd->gkhd/transpose | solution.py:59
  223.5 19.9 %reshape.509 = f32[128,64,512]{2,1,0:T(8,128)} reshape(f32[8,1024,4,128]{3,2,1,0:T(4,128)} %copy.169) | data formatting | bytes 33554432 | tf_op jit(solution)/shard_map/while/body/eval_jaxpr/reshape | solution.py:63
  243.4 37.4 %scatter_fusion.1 = f32[32,64,512]{2,1,0:T(8,128)} fusion(f32[32,64,512]{2,1,0:T(8,128)} %get-tuple-element.301, s32[128]{0:T(128)S(1)} %fusion.90, f32[128,64,512]{2,1,0:T(8,128)} %reshape.509), kind=kCustom, calls=%fused_computation.6.clone.1 | custom fusion | flops 4194304 | bytes 50332160 | tf_op jit(solution)/shard_map/while/body/eval_jaxpr/scatter-add | solution.py:116
  291.1 19.2 %copy.168 = f32[8,1024,4,128]{3,2,1,0:T(4,128)} copy(f32[8,1024,4,128]{1,3,2,0:T(8,128)} %multiply_bitcast_fusion.2) | data formatting | bytes 33554432 | tf_op jit(solution)/shard_map/while/body/eval_jaxpr/mul | solution.py:56
  310.3 19.9 %reshape.508 = f32[128,64,512]{2,1,0:T(8,128)} reshape(f32[8,1024,4,128]{3,2,1,0:T(4,128)} %copy.168) | data formatting | bytes 33554432 | tf_op jit(solution)/shard_map/while/body/eval_jaxpr/reshape | solution.py:62
  330.3 37.2 %scatter_fusion = f32[32,64,512]{2,1,0:T(8,128)} fusion(f32[32,64,512]{2,1,0:T(8,128)} %get-tuple-element.300, s32[128]{0:T(128)S(1)} %fusion.90, f32[128,64,512]{2,1,0:T(8,128)} %reshape.508), kind=kCustom, calls=%fused_computation.5.clone.1 | custom fusion | flops 4194304 | bytes 50332160 | tf_op jit(solution)/shard_map/while/body/eval_jaxpr/scatter-add | solution.py:116
  383.2 12.5 %reshape.506 = bf16[8,1024,4,128]{3,2,1,0:T(4,128)(2,1)} reshape(bf16[128,64,512]{2,1,0:T(8,128)(2,1)} %gather_fusion.1) | data formatting | bytes 16777216 | tf_op jit(solution)/shard_map/while/body/eval_jaxpr/reshape;while/body/eval_jaxpr/reshape | solution.py:26
  403.8 12.5 %reshape.504 = bf16[8,1024,4,128]{3,2,1,0:T(4,128)(2,1)} reshape(bf16[128,64,512]{2,1,0:T(8,128)(2,1)} %gather_fusion) | data formatting | bytes 16777216 | tf_op jit(solution)/shard_map/while/body/eval_jaxpr/reshape;while/body/eval_jaxpr/reshape | solution.py:27
  426.1 12.6 %fusion.93 = (f32[8,4,64]{2,1,0:T(4,128)S(1)}, f32[8,4,64,1024]{3,2,1,0:T(8,128)}) fusion(f32[8,4,64,1024]{3,2,1,0:T(8,128)} %fusion.91, pred[8,64,1024]{2,1,0:T(8,128)(4,1)S(1)} %copy-done.1), kind=kOutput, calls=%fused_computation.108.clone.1 | output fusion | flops 12583935 | bytes 17309696 | tf_op jit(solution)/shard_map/while/body/eval_jaxpr/sub | solution.py:43
  444.1 12.1 %multiply_convert_fusion.2 = bf16[8,4,64,1024]{3,2,1,0:T(8,128)(2,1)} fusion(f32[8,4,64]{2,1,0:T(4,128)S(1)} %fusion.94, f32[8,4,64,1024]{3,2,1,0:T(8,128)} %get-tuple-element.285, f32[8,4,64]{2,1,0:T(4,128)S(1)} %get-tuple-element.286, bf16[8,1024,4,128]{3,2,1,0:T(4,128)(2,1)} %reshape.504, bf16[8,64,4,128]{3,2,1,0:T(4,128)(2,1)S(1)} %reshape.505), kind=kOutput, calls=%fused_computation.12.clone.1 | convolution fusion | flops 545259520 | bytes 21512192 | tf_op jit(solution)/shard_map/while/body/eval_jaxpr/gqhd,gkhd->ghqk/dot_general | solution.py:48
  467.6 11.5 %convolution_bitcast_fusion.2 = f32[8,1024,4,128]{1,3,2,0:T(8,128)} fusion(bf16[8,64,4,128]{3,2,1,0:T(4,128)(2,1)S(1)} %reshape.505, f32[8,4,64,1024]{3,2,1,0:T(8,128)} %get-tuple-element.285, f32[8,4,64]{2,1,0:T(4,128)S(1)} %get-tuple-element.286), kind=kOutput, calls=%fused_computation.11.clone.1 | convolution fusion | flops 541065216 | bytes 25698304 | tf_op jit(solution)/shard_map/while/body/eval_jaxpr/ghqk,gqhd->gkhd/dot_general | solution.py:59
  479.1 19.2 %copy.169 = f32[8,1024,4,128]{3,2,1,0:T(4,128)} copy(f32[8,1024,4,128]{1,3,2,0:T(8,128)} %convolution_bitcast_fusion.2) | data formatting | bytes 33554432 | tf_op jit(solution)/shard_map/while/body/eval_jaxpr/ghqk,gqhd->gkhd/transpose | solution.py:59
  498.3 19.9 %reshape.509 = f32[128,64,512]{2,1,0:T(8,128)} reshape(f32[8,1024,4,128]{3,2,1,0:T(4,128)} %copy.169) | data formatting | bytes 33554432 | tf_op jit(solution)/shard_map/while/body/eval_jaxpr/reshape | solution.py:63
  518.2 38.1 %scatter_fusion.1 = f32[32,64,512]{2,1,0:T(8,128)} fusion(f32[32,64,512]{2,1,0:T(8,128)} %get-tuple-element.301, s32[128]{0:T(128)S(1)} %fusion.90, f32[128,64,512]{2,1,0:T(8,128)} %reshape.509), kind=kCustom, calls=%fused_computation.6.clone.1 | custom fusion | flops 4194304 | bytes 50332160 | tf_op jit(solution)/shard_map/while/body/eval_jaxpr/scatter-add | solution.py:116
  566.6 19.2 %copy.168 = f32[8,1024,4,128]{3,2,1,0:T(4,128)} copy(f32[8,1024,4,128]{1,3,2,0:T(8,128)} %multiply_bitcast_fusion.2) | data formatting | bytes 33554432 | tf_op jit(solution)/shard_map/while/body/eval_jaxpr/mul | solution.py:56
  585.8 19.9 %reshape.508 = f32[128,64,512]{2,1,0:T(8,128)} reshape(f32[8,1024,4,128]{3,2,1,0:T(4,128)} %copy.168) | data formatting | bytes 33554432 | tf_op jit(solution)/shard_map/while/body/eval_jaxpr/reshape | solution.py:62
  605.7 37.8 %scatter_fusion = f32[32,64,512]{2,1,0:T(8,128)} fusion(f32[32,64,512]{2,1,0:T(8,128)} %get-tuple-element.300, s32[128]{0:T(128)S(1)} %fusion.90, f32[128,64,512]{2,1,0:T(8,128)} %reshape.508), kind=kCustom, calls=%fused_computation.5.clone.1 | custom fusion | flops 4194304 | bytes 50332160 | tf_op jit(solution)/shard_map/while/body/eval_jaxpr/scatter-add | solution.py:116
  652.7 10.8 %all-to-all-done.3 = bf16[8,128,512]{2,1,0:T(8,128)(2,1)S(1)} async-done(((bf16[8,128,512]{2,1,0:T(8,128)(2,1)}), bf16[8,128,512]{2,1,0:T(8,128)(2,1)S(1)}, u32[]{:S(2)}, u32[]{:S(2)}) %all-to-all-start.3) | async-done | bytes 1048608 | tf_op jit(solution)/shard_map/all_to_all | solution.py:145
  663.5 10.3 %all-to-all-start.4 = ((f32[16,1,64,512]{3,2,1,0:T(8,128)}), f32[16,1,64,512]{3,2,1,0:T(8,128)}, u32[]{:S(2)}, u32[]{:S(2)}) async-start(f32[16,1,64,512]{3,2,1,0:T(8,128)} %get-tuple-element.188), calls=%async_computation.4 | async-start | bytes 4194304 | tf_op jit(solution)/shard_map/all_to_all | solution.py:122
  678.0 24.4 %all-to-all-done.4 = f32[16,1,64,512]{3,2,1,0:T(8,128)} async-done(((f32[16,1,64,512]{3,2,1,0:T(8,128)}), f32[16,1,64,512]{3,2,1,0:T(8,128)}, u32[]{:S(2)}, u32[]{:S(2)}) %all-to-all-start.4) | async-done | bytes 2097184 | tf_op jit(solution)/shard_map/all_to_all | solution.py:122
  721.8 16.4 %all-to-all-done.6 = f32[16,1,64,512]{3,2,1,0:T(8,128)} async-done(((f32[16,1,64,512]{3,2,1,0:T(8,128)}), f32[16,1,64,512]{3,2,1,0:T(8,128)}, u32[]{:S(2)}, u32[]{:S(2)}) %all-to-all-start.6) | async-done | bytes 2097184 | tf_op jit(solution)/shard_map/all_to_all | solution.py:129
  747.1 11.1 %all-to-all-done.5 = bf16[8,128,512]{2,1,0:T(8,128)(2,1)} async-done(((bf16[8,128,512]{2,1,0:T(8,128)(2,1)}), bf16[8,128,512]{2,1,0:T(8,128)(2,1)}, u32[]{:S(2)}, u32[]{:S(2)}) %all-to-all-start.5) | async-done | bytes 1048608 | tf_op jit(solution)/shard_map/all_to_all | solution.py:147
  766.7 10.9 %all-to-all-done.7 = bf16[8,128,512]{2,1,0:T(8,128)(2,1)S(1)} async-done(((bf16[8,128,512]{2,1,0:T(8,128)(2,1)}), bf16[8,128,512]{2,1,0:T(8,128)(2,1)S(1)}, u32[]{:S(2)}, u32[]{:S(2)}) %all-to-all-start.7) | async-done | bytes 1048608 | tf_op jit(solution)/shard_map/all_to_all | solution.py:155
  (134 shorter events, 206.9 us)
Async XLA Ops:
  0.6 55.1 %copy-start.4 = (s32[16,16]{1,0:T(8,128)S(1)}, s32[16,16]{1,0:T(8,128)}, u32[]{:S(2)}) copy-start(s32[16,16]{1,0:T(8,128)} %param.11) | copy-start | bytes 3076
  0.6 55.1 %copy-start.2 = (bf16[1024,512]{1,0:T(8,128)(2,1)S(1)}, bf16[1024,512]{1,0:T(8,128)(2,1)}, u32[]{:S(2)}) copy-start(bf16[1024,512]{1,0:T(8,128)(2,1)} %param.8) | copy-start | bytes 3145732
  24.0 21.4 %all-to-all-start.1 = ((bf16[16,1,64,512]{3,2,1,0:T(8,128)(2,1)}), bf16[16,1,64,512]{3,2,1,0:T(8,128)(2,1)S(1)}, u32[]{:S(2)}, u32[]{:S(2)}) async-start(bf16[16,1,64,512]{3,2,1,0:T(8,128)(2,1)} %bitcast.19), calls=%async_computation.1 | async-start | bytes 2097152 | tf_op jit(solution)/shard_map/all_to_all | solution.py:90
  45.4 10.4 %copy-start.3 = (bf16[16,1,64,512]{3,2,1,0:T(8,128)(2,1)}, bf16[16,1,64,512]{3,2,1,0:T(8,128)(2,1)S(1)}, u32[]{:S(2)}) copy-start(bf16[16,1,64,512]{3,2,1,0:T(8,128)(2,1)S(1)} %all-to-all-done.1) | copy-start | bytes 3145732
  45.4 22.4 %all-to-all-start.2 = ((bf16[16,1,64,512]{3,2,1,0:T(8,128)(2,1)}), bf16[16,1,64,512]{3,2,1,0:T(8,128)(2,1)}, u32[]{:S(2)}, u32[]{:S(2)}) async-start(bf16[16,1,64,512]{3,2,1,0:T(8,128)(2,1)} %bitcast.23), calls=%async_computation.2 | async-start | bytes 2097152 | tf_op jit(solution)/shard_map/all_to_all | solution.py:91
  141.5 9.8 %copy-start.1 = (pred[8,64,1024]{2,1,0:T(8,128)(4,1)S(1)}, pred[8,64,1024]{2,1,0:T(8,128)(4,1)}, u32[]{:S(2)}) copy-start(pred[8,64,1024]{2,1,0:T(8,128)(4,1)} %or_and_fusion.2) | copy-start | bytes 1572868 | tf_op jit(solution)/shard_map/while
  141.5 22.3 %slice-start = ((s8[8388608]{0:T(1024)(128)(4,1)}), s8[4194304]{0:T(1024)(128)(4,1)S(1)}, s32[]{:S(2)}) async-start(s8[8388608]{0:T(1024)(128)(4,1)} %bitcast.120), calls=%async_computation.8 | async-start | bytes 8388608 | tf_op jit(solution)/shard_map/while
  151.3 12.6 %slice-start.1 = ((s8[8388608]{0:T(1024)(128)(4,1)}), s8[4194304]{0:T(1024)(128)(4,1)S(1)}, s32[]{:S(2)}) async-start(s8[8388608]{0:T(1024)(128)(4,1)} %bitcast.120), calls=%async_computation.9 | async-start | bytes 8388608 | tf_op jit(solution)/shard_map/while
  151.3 12.6 %copy-start = (f32[8,4,64,128]{3,1,2,0:T(4,128)S(1)}, f32[8,4,64,128]{3,1,2,0:T(4,128)}, u32[]{:S(2)}) copy-start(f32[8,4,64,128]{3,1,2,0:T(4,128)} %bitcast_convert_fusion.2) | copy-start | bytes 3145732 | tf_op jit(solution)/shard_map/while
  416.3 9.8 %copy-start.1 = (pred[8,64,1024]{2,1,0:T(8,128)(4,1)S(1)}, pred[8,64,1024]{2,1,0:T(8,128)(4,1)}, u32[]{:S(2)}) copy-start(pred[8,64,1024]{2,1,0:T(8,128)(4,1)} %or_and_fusion.2) | copy-start | bytes 1572868 | tf_op jit(solution)/shard_map/while
  416.3 22.3 %slice-start = ((s8[8388608]{0:T(1024)(128)(4,1)}), s8[4194304]{0:T(1024)(128)(4,1)S(1)}, s32[]{:S(2)}) async-start(s8[8388608]{0:T(1024)(128)(4,1)} %bitcast.120), calls=%async_computation.8 | async-start | bytes 8388608 | tf_op jit(solution)/shard_map/while
  426.1 12.6 %slice-start.1 = ((s8[8388608]{0:T(1024)(128)(4,1)}), s8[4194304]{0:T(1024)(128)(4,1)S(1)}, s32[]{:S(2)}) async-start(s8[8388608]{0:T(1024)(128)(4,1)} %bitcast.120), calls=%async_computation.9 | async-start | bytes 8388608 | tf_op jit(solution)/shard_map/while
  426.1 12.6 %copy-start = (f32[8,4,64,128]{3,1,2,0:T(4,128)S(1)}, f32[8,4,64,128]{3,1,2,0:T(4,128)}, u32[]{:S(2)}) copy-start(f32[8,4,64,128]{3,1,2,0:T(4,128)} %bitcast_convert_fusion.2) | copy-start | bytes 3145732 | tf_op jit(solution)/shard_map/while
  643.5 20.0 %all-to-all-start.3 = ((bf16[8,128,512]{2,1,0:T(8,128)(2,1)}), bf16[8,128,512]{2,1,0:T(8,128)(2,1)S(1)}, u32[]{:S(2)}, u32[]{:S(2)}) async-start(bf16[8,128,512]{2,1,0:T(8,128)(2,1)} %bitcast.132), calls=%async_computation.3 | async-start | bytes 2097152 | tf_op jit(solution)/shard_map/all_to_all | solution.py:145
  663.5 46.0 %copy-start.5 = (s32[16]{0:T(128)S(1)}, s32[16]{0:T(128)}, u32[]{:S(2)}) copy-start(s32[16]{0:T(128)} %get-tuple-element.154) | copy-start | bytes 196
  663.5 38.9 %all-to-all-start.4 = ((f32[16,1,64,512]{3,2,1,0:T(8,128)}), f32[16,1,64,512]{3,2,1,0:T(8,128)}, u32[]{:S(2)}, u32[]{:S(2)}) async-start(f32[16,1,64,512]{3,2,1,0:T(8,128)} %get-tuple-element.188), calls=%async_computation.4 | async-start | bytes 4194304 | tf_op jit(solution)/shard_map/all_to_all | solution.py:122
  702.4 35.7 %all-to-all-start.6 = ((f32[16,1,64,512]{3,2,1,0:T(8,128)}), f32[16,1,64,512]{3,2,1,0:T(8,128)}, u32[]{:S(2)}, u32[]{:S(2)}) async-start(f32[16,1,64,512]{3,2,1,0:T(8,128)} %get-tuple-element.186), calls=%async_computation.6 | async-start | bytes 4194304 | tf_op jit(solution)/shard_map/all_to_all | solution.py:129
  738.1 20.1 %all-to-all-start.5 = ((bf16[8,128,512]{2,1,0:T(8,128)(2,1)}), bf16[8,128,512]{2,1,0:T(8,128)(2,1)}, u32[]{:S(2)}, u32[]{:S(2)}) async-start(bf16[8,128,512]{2,1,0:T(8,128)(2,1)} %bitcast_dynamic-update-slice_fusion), calls=%async_computation.5 | async-start | bytes 2097152 | tf_op jit(solution)/shard_map/all_to_all | solution.py:147
  758.2 19.3 %all-to-all-start.7 = ((bf16[8,128,512]{2,1,0:T(8,128)(2,1)}), bf16[8,128,512]{2,1,0:T(8,128)(2,1)S(1)}, u32[]{:S(2)}, u32[]{:S(2)}) async-start(bf16[8,128,512]{2,1,0:T(8,128)(2,1)} %bitcast.43), calls=%async_computation.7 | async-start | bytes 2097152 | tf_op jit(solution)/shard_map/all_to_all | solution.py:155
